TPU v7x, 128 devices: a whole 4x4x4 slice. The times are simulated.
128 devices in a mesh: cfg: 2 (over core), lat: 4 (over x), seq: 16 (over z, y).
Axes of the slice: x: 4, y: 4, z: 4, core: 2. Of those that a mesh axis runs over, the one named last changes fastest.
Arguments:
- latents: float32 [24, 1024, 16], P('lat', 'seq'), may hold values from -6 to 6
- timesteps: int32 [24], P('lat'), may hold values from 0 to 999
- labels: int32 [24], P('lat'), may hold values from 0 to 999
- guidance: float32 [1], replicated, may hold values from 1.5 to 4
- keep_coef: float32 [24], P('lat'), may hold values from 0.8 to 1.2
- noise_coef: float32 [24], P('lat'), may hold values from -0.6 to -0.2
- w_patch: bfloat16 [16, 1152], replicated, may hold values from -1.5 to 1.5
- label_table: bfloat16 [1001, 1152], replicated, may hold values from -6 to 6
- w_time1: bfloat16 [256, 1152], P(None, 'lat'), may hold values from -0.375 to 0.375
- w_time2: bfloat16 [1152, 1152], P(None, 'lat'), may hold values from -0.1875 to 0.1875
- ada_weight: bfloat16 [1152, 9216], P(None, 'seq'), may hold values from -0.1875 to 0.1875
- w_qkv: bfloat16 [1152, 3456], P(None, 'seq'), may hold values from -2.9168155 to 2.9168155
- w_proj: bfloat16 [1152, 1152], P(None, 'seq'), may hold values from -0.1875 to 0.1875
- w_fc1: bfloat16 [1152, 4608], P(None, 'seq'), may hold values from -0.1875 to 0.1875
- w_fc2: bfloat16 [4608, 1152], P('seq'), may hold values from -0.09375 to 0.09375
- w_out: bfloat16 [1152, 16], replicated, may hold values from -0.1875 to 0.1875
Outputs:
- next_latents: float32 [24, 1024, 16], P('lat', 'seq', 'cfg')
All inputs are finite; a program needn't handle non-finite values.
Results may differ from a plain program's by a relative error of at most 0.009.
Values may be sent and summed in bfloat16 or wider, within the bound.
A program may use at most 192 MiB of HBM per device.

v0:
```python
import math
import jax
import jax.numpy as jnp
from jax import lax
from jax.sharding import PartitionSpec as P

D = 1152
HEADS = 16
HEAD_DIM = 72
CLASSES = 1000
FREQ = 256
GRID = 32


def swapped(value, axis, stride):
    mask = 2**stride
    pairs = [(source, source ^ mask) for source in range(lax.axis_size(axis))]
    return lax.ppermute(value, axis, pairs)


def layer_norm(values):
    average = jnp.mean(values, axis=-1, keepdims=True)
    centered = values - average
    spread = jnp.mean(centered * centered, axis=-1, keepdims=True)
    return centered * lax.rsqrt(spread + 1e-06)


def modulate(values, shifted, scaled):
    return layer_norm(values) * (1.0 + scaled[:, None, :]) + shifted[:, None, :]


def time_waves(timesteps):
    half_count = FREQ // 2
    frequency = jnp.exp(-math.log(10000.0) * jnp.arange(half_count, dtype=jnp.float32) / half_count)
    angles = timesteps.astype(jnp.float32)[:, None] * frequency[None, :]
    return jnp.concatenate([jnp.cos(angles), jnp.sin(angles)], axis=-1)


def grid_waves(positions):
    quarter = D // 4
    frequency = jnp.exp(-math.log(10000.0) * jnp.arange(quarter, dtype=jnp.float32) / quarter)
    column = (positions % GRID).astype(jnp.float32)[:, None] * frequency[None, :]
    row_angle = (positions // GRID).astype(jnp.float32)[:, None] * frequency[None, :]
    return jnp.concatenate(
        [jnp.sin(column), jnp.cos(column), jnp.sin(row_angle), jnp.cos(row_angle)], axis=-1
    )


def condition(timesteps, classes, label_table, w_time1, w_time2):
    waves = time_waves(timesteps).astype(jnp.bfloat16)
    hidden_time = jax.nn.silu(jnp.dot(waves, w_time1, preferred_element_type=jnp.float32)).astype(
        jnp.bfloat16
    )
    time_vector = jnp.dot(hidden_time, w_time2, preferred_element_type=jnp.float32)
    onehot = (classes[:, None] == jnp.arange(CLASSES + 1, dtype=jnp.int32)[None, :]).astype(
        jnp.bfloat16
    )
    return time_vector + jnp.dot(onehot, label_table, preferred_element_type=jnp.float32)


def shards(
    latents,
    timesteps,
    labels,
    guidance,
    keep_coef,
    noise_coef,
    w_patch,
    label_table,
    w_time1,
    w_time2,
    ada_weight,
    w_qkv,
    w_proj,
    w_fc1,
    w_fc2,
    w_out,
):
    lat_count, tok_count, channels = latents.shape
    model_width = w_patch.shape[1]
    side_index = lax.axis_index("cfg")
    classes = jnp.where(side_index == 0, labels, CLASSES)
    time_first, time_second = (
        lax.all_gather(w_time1, "lat", axis=1, tiled=True),
        lax.all_gather(w_time2, "lat", axis=1, tiled=True),
    )
    conditioning = condition(timesteps, classes, label_table, time_first, time_second)
    own_columns = jnp.dot(
        jax.nn.silu(conditioning).astype(jnp.bfloat16),
        ada_weight,
        preferred_element_type=jnp.float32,
    )
    modulation = lax.all_gather(own_columns, "seq", axis=1, tiled=True)
    pieces = [
        modulation[:, number * model_width : (number + 1) * model_width] for number in range(8)
    ]
    positions = lax.axis_index("seq") * tok_count + jnp.arange(tok_count, dtype=jnp.int32)
    state = jnp.dot(
        latents.reshape(-1, channels).astype(jnp.bfloat16),
        w_patch,
        preferred_element_type=jnp.float32,
    )
    state = state.reshape(lat_count, tok_count, model_width) + grid_waves(positions)[None]
    qkv_full, proj_full = (
        lax.all_gather(w_qkv, "seq", axis=1, tiled=True),
        lax.all_gather(w_proj, "seq", axis=1, tiled=True),
    )
    normed = modulate(state, pieces[0], pieces[1]).astype(jnp.bfloat16).reshape(-1, model_width)
    triple = jnp.dot(normed, qkv_full, preferred_element_type=jnp.float32).astype(jnp.bfloat16)
    queries = triple[:, :model_width].reshape(lat_count, tok_count, HEADS, HEAD_DIM)
    keys_own = triple[:, model_width : 2 * model_width].reshape(lat_count, tok_count, model_width)
    values_own = triple[:, 2 * model_width :].reshape(lat_count, tok_count, model_width)
    factor = 1.0 / math.sqrt(HEAD_DIM)
    row_best = jnp.full((lat_count, HEADS, tok_count), -1e30, jnp.float32)
    keys_part = lax.all_gather(keys_own, "seq", axis=1, tiled=True)
    values_part = lax.all_gather(values_own, "seq", axis=1, tiled=True)
    key_count = keys_part.shape[1]
    keys_heads = keys_part.reshape(lat_count, key_count, HEADS, HEAD_DIM)
    values_heads = values_part.reshape(lat_count, key_count, HEADS, HEAD_DIM)
    scores = (
        jnp.einsum("lqhd,lkhd->lhqk", queries, keys_heads, preferred_element_type=jnp.float32)
        * factor
    )
    raised = jnp.maximum(row_best, jnp.max(scores, axis=-1))
    exponent = jnp.exp(scores - raised[..., None])
    row_sums = jnp.sum(exponent, axis=-1)
    weighted = jnp.einsum(
        "lhqk,lkhd->lhqd",
        exponent.astype(jnp.bfloat16),
        values_heads,
        preferred_element_type=jnp.float32,
    )
    row_best, row_sums, weighted = (raised, row_sums, weighted)
    attended = (
        (weighted / row_sums[..., None])
        .transpose(0, 2, 1, 3)
        .reshape(-1, model_width)
        .astype(jnp.bfloat16)
    )
    projected = jnp.dot(attended, proj_full, preferred_element_type=jnp.float32)
    state = state + pieces[2][:, None, :] * projected.reshape(lat_count, tok_count, model_width)
    normed = modulate(state, pieces[3], pieces[4]).astype(jnp.bfloat16).reshape(-1, model_width)
    fc1_full, fc2_full = (
        lax.all_gather(w_fc1, "seq", axis=1, tiled=True),
        lax.all_gather(w_fc2, "seq", axis=0, tiled=True),
    )
    hidden = jax.nn.gelu(
        jnp.dot(normed, fc1_full, preferred_element_type=jnp.float32), approximate=True
    ).astype(jnp.bfloat16)
    mlp_out = jnp.dot(hidden, fc2_full, preferred_element_type=jnp.float32)
    state = state + pieces[5][:, None, :] * mlp_out.reshape(lat_count, tok_count, model_width)
    final = modulate(state, pieces[6], pieces[7]).astype(jnp.bfloat16).reshape(-1, model_width)
    noise_own = jnp.dot(final, w_out, preferred_element_type=jnp.float32).reshape(
        lat_count, tok_count, channels
    )
    half_width = channels // 2
    own_latent = lax.dynamic_slice_in_dim(latents, side_index * half_width, half_width, 2)
    partner = swapped(noise_own, "cfg", 0)
    cond_noise = jnp.where(side_index == 0, noise_own, partner)
    free_noise = jnp.where(side_index == 0, partner, noise_own)
    combined = free_noise + guidance[0] * (cond_noise - free_noise)
    guided = lax.dynamic_slice_in_dim(combined, side_index * half_width, half_width, 2)
    return keep_coef[:, None, None] * own_latent + noise_coef[:, None, None] * guided


def solution(mesh):
    return jax.shard_map(
        shards,
        mesh=mesh,
        in_specs=(
            P("lat", "seq", None),
            P("lat"),
            P("lat"),
            P(),
            P("lat"),
            P("lat"),
            P(),
            P(),
            P(None, "lat"),
            P(None, "lat"),
            P(None, "seq"),
            P(None, "seq"),
            P(None, "seq"),
            P(None, "seq"),
            P("seq", None),
            P(),
        ),
        out_specs=P("lat", "seq", "cfg"),
        check_vma=False,
    )
```

profile of v0, /device:TPU:1, one launch (start us, length us, event | category | flops | bytes accessed | tf_op | source)
XLA Modules:
  0.0 571.2 jit_solution(164010904563712114)
XLA Ops:
  9.7 1.3 fusion.61
  12.6 12.5 %all_gather.27 = bf16[256,1152]{0,1:T(8,128)(2,1)S(1)} all-gather(bf16[256,288]{0,1:T(8,128)(2,1)S(1)} %copy-done.5), channel_id=1, replica_groups=mesh['cfg'=2,'lat'=4,'seq'=16] {'lat'}, dimensions={1}, use_global_device_ids=true | all-gather | bytes 737280 | tf_op jit(solution)/shard_map/all_gather | solution.py:84
  25.2 23.4 %all-gather.9.cloned.1.call-done = bf16[1152,1152]{0,1:T(8,128)(2,1)} async-done(((bf16[1152,288]{0,1:T(8,128)(2,1)}), bf16[1152,1152]{0,1:T(8,128)(2,1)}) %all-gather.9.cloned.1.call-update) | async-done | bytes 2654224 | tf_op jit(solution)/shard_map/all_gather | solution.py:85
  48.6 2.7 fusion.31
  51.3 2.1 convolution_bitcast_fusion
  53.5 21.0 %all-gather = f32[16,576,6]{1,2,0:T(8,128)S(1)} all-gather(f32[1,576,6]{1,2,0:T(8,128)S(1)} %convolution_bitcast_fusion), channel_id=1, replica_groups=mesh['cfg'=2,'lat'=4,'seq'=16] {'seq'}, dimensions={0}, use_global_device_ids=true | all-gather | bytes 235008 | tf_op jit(solution)/shard_map/all_gather | solution.py:93
  75.1 45.3 %all-gather.11.cloned.1.call-done = bf16[1152,3456]{0,1:T(8,128)(2,1)} async-done(((bf16[1152,216]{0,1:T(8,128)(2,1)}), bf16[1152,3456]{0,1:T(8,128)(2,1)}) %all-gather.11.cloned.1.call-update) | async-done | bytes 7962640 | tf_op jit(solution)/shard_map/all_gather | solution.py:105
  120.4 8.3 %convolution_convert_fusion = bf16[384,3456]{1,0:T(8,128)(2,1)S(1)} fusion(bf16[384,1152]{1,0:T(8,128)(2,1)S(1)} %bitcast.55, bf16[1152,3456]{0,1:T(8,128)(2,1)} %all-gather.11.cloned.1.call-done), kind=kOutput, calls=%fused_computation.16 | convolution fusion | flops 3058974720 | bytes 11501568 | tf_op jit(solution)/shard_map/dot_general | solution.py:109
  128.7 1.5 fusion.60
  132.6 3.6 reshape.137
  136.3 91.6 %all-gather.13.cloned.1.call-done = bf16[6,1024,1152]{2,1,0:T(8,128)(2,1)} async-done(((bf16[6,64,1152]{2,1,0:T(8,128)(2,1)}), bf16[6,1024,1152]{2,1,0:T(8,128)(2,1)}) %all-gather.13.cloned.1.call-update) | async-done | bytes 14155792 | tf_op jit(solution)/shard_map/all_gather | solution.py:115
  227.9 18.7 %copy.27 = bf16[6,1024,1152]{1,2,0:T(8,128)(2,1)} copy(bf16[6,1024,1152]{2,1,0:T(8,128)(2,1)} %all-gather.13.cloned.1.call-done) | data formatting | bytes 28311552 | tf_op jit(solution)/shard_map/all_gather | solution.py:115
  246.7 80.9 %all-gather.15.cloned.1.call-done = bf16[6,1024,1152]{2,1,0:T(8,128)(2,1)} async-done(((bf16[6,64,1152]{2,1,0:T(8,128)(2,1)}), bf16[6,1024,1152]{2,1,0:T(8,128)(2,1)}) %all-gather.15.cloned.1.call-update) | async-done | bytes 14155792 | tf_op jit(solution)/shard_map/all_gather | solution.py:116
  327.6 18.7 %copy.29 = bf16[6,1024,1152]{1,2,0:T(8,128)(2,1)} copy(bf16[6,1024,1152]{2,1,0:T(8,128)(2,1)} %all-gather.15.cloned.1.call-done) | data formatting | bytes 28311552 | tf_op jit(solution)/shard_map/all_gather | solution.py:116
  346.3 18.5 %multiply_reduce_fusion = (f32[6,16,64]{2,1,0:T(8,128)S(1)}, f32[6,16,64,1024]{3,2,1,0:T(8,128)}) fusion(bf16[6,1024,16,72]{1,3,2,0:T(8,128)(2,1)} %bitcast.48, bf16[6,64,16,72]{3,2,1,0:T(8,128)(2,1)} %reshape.137), kind=kOutput, calls=%fused_computation.1 | convolution fusion | flops 918546432 | bytes 40230912 | tf_op jit(solution)/shard_map/lqhd,lkhd->lhqk/dot_general | solution.py:121
  364.8 11.2 %fusion = f32[6,16,64]{2,1,0:T(8,128)S(1)} fusion(f32[6,16,64,1024]{3,2,1,0:T(8,128)} %get-tuple-element.29, f32[6,16,64]{2,1,0:T(8,128)S(1)} %broadcast_maximum_fusion), kind=kLoop, calls=%fused_computation.2 | loop fusion | flops 18868224 | bytes 25214976 | tf_op jit(solution)/shard_map/reduce_sum | solution.py:126
  376.0 14.7 %fusion.20 = bf16[6,64,16,72]{3,1,2,0:T(8,128)(2,1)S(1)} fusion(bf16[6,1024,16,72]{1,3,2,0:T(8,128)(2,1)} %bitcast.49, f32[6,16,64,1024]{3,2,1,0:T(8,128)} %get-tuple-element.29, f32[6,16,64]{2,1,0:T(8,128)S(1)} %broadcast_maximum_fusion, f32[6,64,16]{1,2,0:T(8,128)S(1)} %bitcast.56), kind=kOutput, calls=%fused_computation.25 | convolution fusion | flops 925728768 | bytes 40255488 | tf_op jit(solution)/shard_map/lhqk,lkhd->lhqd/dot_general | solution.py:127
  390.8 2.2 copy.30
  393.0 3.2 convert_element_type.64
  396.2 3.3 fusion.62
  401.3 56.8 %all-gather.19.cloned.1.call-done = bf16[1152,4608]{0,1:T(8,128)(2,1)} async-done(((bf16[1152,288]{0,1:T(8,128)(2,1)}), bf16[1152,4608]{0,1:T(8,128)(2,1)}) %all-gather.19.cloned.1.call-update) | async-done | bytes 10616848 | tf_op jit(solution)/shard_map/all_gather | solution.py:144
  458.1 82.9 %all-gather.21.cloned.1.call-done = bf16[4608,1152]{1,0:T(8,128)(2,1)} async-done(((bf16[288,1152]{1,0:T(8,128)(2,1)}), bf16[4608,1152]{1,0:T(8,128)(2,1)}) %all-gather.21.cloned.1.call-update) | async-done | bytes 10616848 | tf_op jit(solution)/shard_map/all_gather | solution.py:145
  540.9 17.6 %fusion.14 = f32[384,1152]{1,0:T(8,128)} fusion(bf16[4608,1152]{1,0:T(8,128)(2,1)} %all-gather.21.cloned.1.call-done, bf16[384,1152]{1,0:T(8,128)(2,1)S(1)} %bitcast.54, bf16[1152,4608]{0,1:T(8,128)(2,1)} %all-gather.19.cloned.1.call-done), kind=kOutput, calls=%fused_computation.17 | convolution fusion | flops 8169652224 | bytes 23887872 | tf_op jit(solution)/shard_map/dot_general | solution.py:150
  558.6 2.5 fusion.59
  (64 shorter events, 12.1 us)
Async XLA Ops:
  6.5 44.8 %copy-start = (bf16[1001,1152]{1,0:T(8,128)(2,1)S(1)}, bf16[1001,1152]{1,0:T(8,128)(2,1)}, u32[]{:S(2)}) copy-start(bf16[1001,1152]{1,0:T(8,128)(2,1)} %param.23) | copy-start | bytes 6918916
  6.5 3.2 copy-start.6
  6.5 42.0 %all-gather.9.cloned.1.call-start = ((), (), s32[]{:S(2)}) async-start(), calls=%async_computation | async-start | bytes 3317760 | tf_op jit(solution)/shard_map/all_gather | solution.py:85
  7.3 113.1 %all-gather.11.cloned.1.call-start = ((), (), s32[]{:S(2)}) async-start(), calls=%async_computation.1 | async-start | bytes 8460288 | tf_op jit(solution)/shard_map/all_gather | solution.py:105
  8.0 219.9 %all-gather.13.cloned.1.call-start = ((), (), s32[]{:S(2)}) async-start(), calls=%async_computation.2 | async-start | bytes 15040512 | tf_op jit(solution)/shard_map/all_gather | solution.py:115
  9.5 3.0 copy-start.5
  9.7 15.3 %copy-start.10 = (s32[6]{0:T(128)S(1)}, s32[6]{0:T(128)}, u32[]{:S(2)}) copy-start(s32[6]{0:T(128)} %param.18) | copy-start | bytes 76
  11.0 1.2 copy-start.2
  53.5 21.2 %copy-start.3 = (f32[6,64,1152]{2,1,0:T(8,128)S(1)}, f32[6,64,1152]{2,1,0:T(8,128)}, u32[]{:S(2)}) copy-start(f32[6,64,1152]{2,1,0:T(8,128)} %copy-done.2) | copy-start | bytes 5308420
  130.2 197.4 %all-gather.15.cloned.1.call-start = ((), (), s32[]{:S(2)}) async-start(), calls=%async_computation.3 | async-start | bytes 15040512 | tf_op jit(solution)/shard_map/all_gather | solution.py:116
  130.7 265.5 %all-gather.17.cloned.1.call-start = ((), (), s32[]{:S(2)}) async-start(), calls=%async_computation.4 | async-start | bytes 2820096 | tf_op jit(solution)/shard_map/all_gather | solution.py:106
  131.3 326.7 %all-gather.19.cloned.1.call-start = ((), (), s32[]{:S(2)}) async-start(), calls=%async_computation.5 | async-start | bytes 11280384 | tf_op jit(solution)/shard_map/all_gather | solution.py:144
  131.9 409.0 %all-gather.21.cloned.1.call-start = ((), (), s32[]{:S(2)}) async-start(), calls=%async_computation.6 | async-start | bytes 11280384 | tf_op jit(solution)/shard_map/all_gather | solution.py:145
  399.6 1.3 copy-start.4
  558.6 2.9 copy-start.9
  558.6 5.7 %copy-start.1 = (bf16[1001,1152]{1,0:T(8,128)(2,1)S(1)}, bf16[1001,1152]{1,0:T(8,128)(2,1)}, u32[]{:S(2)}) copy-start(bf16[1001,1152]{1,0:T(8,128)(2,1)} %param.23) | copy-start | bytes 6918916
  561.1 2.5 copy-start.7
  561.1 2.5 copy-start.8
  562.0 1.6 collective-permute-start
Sparse Core Ops, SparseCore 0:
  9.0 39.5 all-gather.8
  50.7 69.6 all-gather.10
  130.3 97.5 all-gather.12
  229.9 97.6 all-gather.14
  329.6 45.8 all-gather.16
  377.4 80.5 all-gather.18
  460.2 80.6 all-gather.20
where the time goes:
time: 573 us; the launch traced here: 571 us
  waiting for transfers between devices  385 us (67%)
  matrix products  69.3 us (12%)
  local copies, waits for them, and re-layouts  50.5 us (9%)
  blocking collectives  33.4 us (6%)
  other arithmetic  17.8 us (3%)
  between operations  14.4 us (3%)
    all_gather x1, waiting for transfers between devices, shards(): keys_part = lax.all_gather(keys_own, 'seq', axis=1, tiled=True)  91.6 us
    all_gather x1, waiting for transfers between devices, shards(): lax.all_gather(w_fc2, 'seq', axis=0, tiled=True)  82.9 us
    all_gather x1, waiting for transfers between devices, shards(): values_part = lax.all_gather(values_own, 'seq', axis=1, tiled=True)  80.9 us
    all_gather x1, waiting for transfers between devices, shards(): lax.all_gather(w_fc1, 'seq', axis=1, tiled=True)  56.8 us
    all_gather x1, waiting for transfers between devices, shards(): lax.all_gather(w_qkv, 'seq', axis=1, tiled=True)  45.3 us
    all_gather x1, waiting for transfers between devices, shards(): lax.all_gather(w_time2, 'lat', axis=1, tiled=True)  23.4 us
    all_gather x1, blocking collectives, shards(): modulation = lax.all_gather(own_columns, 'seq', axis=1, tiled=True)  21 us
    all_gather x1, local copies, waits for them, and re-layouts, shards(): keys_part = lax.all_gather(keys_own, 'seq', axis=1, tiled=True)  18.7 us
  transfers between devices with their start and end apart: 8, of which 7 were waited for; matrix products, arithmetic and copies ran while one was open for 18% of the time, Pallas kernels for 0%

commit v1 on v0

--- a/solution.py
+++ b/solution.py
@@ -112,8 +112,11 @@
     values_own = triple[:, 2 * model_width :].reshape(lat_count, tok_count, model_width)
     factor = 1.0 / math.sqrt(HEAD_DIM)
     row_best = jnp.full((lat_count, HEADS, tok_count), -1e30, jnp.float32)
-    keys_part = lax.all_gather(keys_own, "seq", axis=1, tiled=True)
-    values_part = lax.all_gather(values_own, "seq", axis=1, tiled=True)
+    keys_part, values_part = jnp.split(
+        lax.all_gather(jnp.concatenate([keys_own, values_own], axis=0), "seq", axis=1, tiled=True),
+        [keys_own.shape[0]],
+        axis=0,
+    )
     key_count = keys_part.shape[1]
     keys_heads = keys_part.reshape(lat_count, key_count, HEADS, HEAD_DIM)
     values_heads = values_part.reshape(lat_count, key_count, HEADS, HEAD_DIM)

time: 573 us -> 545 us (0.951)
  waiting for transfers between devices: 385 us -> 336 us
  local copies, waits for them, and re-layouts: 50.5 us -> 69.5 us
    split x0 -> x3, local copies, waits for them, and re-layouts: none -> 57.6 us  [shards(): jnp.split(lax.all_gather(jnp.concatenate([keys_own, values_own], axis=0),...]
    all_gather x1, waiting for transfers between devices: 56.8 us -> 16.7 us  [shards(): lax.all_gather(w_fc1, 'seq', axis=1, tiled=True)]
    all_gather x2 -> x0, local copies, waits for them, and re-layouts: 37.4 us -> none  [the longest x1 18.7 us: shards(): keys_part = lax.all_gather(keys_own, 'seq', axis=1, tiled=True)]
    all_gather x2 -> x1, waiting for transfers between devices: 173 us -> 165 us  [shards(): lax.all_gather(jnp.concatenate([keys_own, values_own], axis=0), 'seq', ax...]
  transfers between devices with their start and end apart: 8 -> 7, of which waited for: 7 -> 6; matrix products, arithmetic and copies ran while one was open for 18% -> 23% of each run, Pallas kernels for 0% -> 0%
where the time goes in v1:
time: 545 us; the launch traced here: 544 us
  waiting for transfers between devices  336 us (62%)
  matrix products  70.1 us (13%)
  local copies, waits for them, and re-layouts  69.5 us (13%)
  blocking collectives  33.5 us (6%)
  other arithmetic  19.6 us (4%)
  between operations  14.4 us (3%)
    all_gather x1, waiting for transfers between devices, shards(): lax.all_gather(jnp.concatenate([keys_own, values_own], axis=0), 'seq', ax...  165 us
    all_gather x1, waiting for transfers between devices, shards(): lax.all_gather(w_fc2, 'seq', axis=0, tiled=True)  82.7 us
    split x3, local copies, waits for them, and re-layouts, shards(): jnp.split(lax.all_gather(jnp.concatenate([keys_own, values_own], axis=0),...  57.6 us
    all_gather x1, waiting for transfers between devices, shards(): lax.all_gather(w_qkv, 'seq', axis=1, tiled=True)  45.3 us
    all_gather x1, waiting for transfers between devices, shards(): lax.all_gather(w_time2, 'lat', axis=1, tiled=True)  23.4 us
    all_gather x1, blocking collectives, shards(): modulation = lax.all_gather(own_columns, 'seq', axis=1, tiled=True)  21 us
    dot_general x1, matrix products, shards(): jnp.einsum('lqhd,lkhd->lhqk', queries, keys_heads, preferred_element_type...  19.1 us
    dot_general x1, matrix products, shards(): mlp_out = jnp.dot(hidden, fc2_full, preferred_element_type=jnp.float32)  17.6 us
  transfers between devices with their start and end apart: 7, of which 6 were waited for; matrix products, arithmetic and copies ran while one was open for 23% of the time, Pallas kernels for 0%

profile of v1, /device:TPU:1, one launch (start us, length us, event | category | flops | bytes accessed | tf_op | source)
XLA Modules:
  0.0 543.8 jit_solution(13782747618091548766)
XLA Ops:
  9.7 1.3 fusion.62
  12.5 12.5 %all_gather.24 = bf16[256,1152]{0,1:T(8,128)(2,1)S(1)} all-gather(bf16[256,288]{0,1:T(8,128)(2,1)S(1)} %copy-done.5), channel_id=1, replica_groups=mesh['cfg'=2,'lat'=4,'seq'=16] {'lat'}, dimensions={1}, use_global_device_ids=true | all-gather | bytes 737280 | tf_op jit(solution)/shard_map/all_gather | solution.py:84
  25.2 23.4 %all-gather.8.cloned.1.call-done = bf16[1152,1152]{0,1:T(8,128)(2,1)} async-done(((bf16[1152,288]{0,1:T(8,128)(2,1)}), bf16[1152,1152]{0,1:T(8,128)(2,1)}) %all-gather.8.cloned.1.call-update) | async-done | bytes 2654224 | tf_op jit(solution)/shard_map/all_gather | solution.py:85
  48.6 2.7 fusion.31
  51.3 2.1 convolution_bitcast_fusion
  53.5 21.0 %all-gather = f32[16,576,6]{1,2,0:T(8,128)S(1)} all-gather(f32[1,576,6]{1,2,0:T(8,128)S(1)} %convolution_bitcast_fusion), channel_id=1, replica_groups=mesh['cfg'=2,'lat'=4,'seq'=16] {'seq'}, dimensions={0}, use_global_device_ids=true | all-gather | bytes 235008 | tf_op jit(solution)/shard_map/all_gather | solution.py:93
  75.1 45.3 %all-gather.10.cloned.1.call-done = bf16[1152,3456]{0,1:T(8,128)(2,1)} async-done(((bf16[1152,216]{0,1:T(8,128)(2,1)}), bf16[1152,3456]{0,1:T(8,128)(2,1)}) %all-gather.10.cloned.1.call-update) | async-done | bytes 7962640 | tf_op jit(solution)/shard_map/all_gather | solution.py:105
  120.4 8.3 %convolution_convert_fusion = bf16[384,3456]{1,0:T(8,128)(2,1)S(1)} fusion(bf16[384,1152]{1,0:T(8,128)(2,1)S(1)} %bitcast.55, bf16[1152,3456]{0,1:T(8,128)(2,1)} %all-gather.10.cloned.1.call-done), kind=kOutput, calls=%fused_computation.16 | convolution fusion | flops 3058974720 | bytes 11501568 | tf_op jit(solution)/shard_map/dot_general | solution.py:109
  128.9 1.4 pad_maximum_fusion
  132.0 3.7 reshape.137
  135.7 164.7 %all-gather.12.cloned.1.call-done = bf16[12,1024,1152]{2,1,0:T(8,128)(2,1)} async-done(((bf16[12,64,1152]{2,1,0:T(8,128)(2,1)}), bf16[12,1024,1152]{2,1,0:T(8,128)(2,1)}) %all-gather.12.cloned.1.call-update) | async-done | bytes 28311568 | tf_op jit(solution)/shard_map/all_gather | solution.py:116
  300.4 20.2 %fusion.60 = (bf16[6,1024,1152]{2,1,0:T(8,128)(2,1)}, bf16[6,1024,1152]{2,1,0:T(8,128)(2,1)}) fusion(bf16[12,1024,1152]{2,1,0:T(8,128)(2,1)} %all-gather.12.cloned.1.call-done), kind=kLoop, calls=%fused_computation.94 | loop fusion | bytes 56623104 | tf_op jit(solution)/shard_map/split | solution.py:115
  320.6 18.7 %copy.27 = bf16[6,1024,1152]{1,2,0:T(8,128)(2,1)} copy(bf16[6,1024,1152]{2,1,0:T(8,128)(2,1)} %get-tuple-element.7) | data formatting | bytes 28311552 | tf_op jit(solution)/shard_map/split | solution.py:115
  339.3 18.7 %copy.29 = bf16[6,1024,1152]{1,2,0:T(8,128)(2,1)} copy(bf16[6,1024,1152]{2,1,0:T(8,128)(2,1)} %get-tuple-element.8) | data formatting | bytes 28311552 | tf_op jit(solution)/shard_map/split | solution.py:115
  358.0 19.1 %multiply_reduce_fusion = (f32[6,16,64]{2,1,0:T(8,128)S(1)}, f32[6,16,64,1024]{3,2,1,0:T(8,128)}) fusion(bf16[6,1024,16,72]{1,3,2,0:T(8,128)(2,1)} %bitcast.48, bf16[6,64,16,72]{3,2,1,0:T(8,128)(2,1)} %reshape.137), kind=kOutput, calls=%fused_computation.1 | convolution fusion | flops 918546432 | bytes 40230912 | tf_op jit(solution)/shard_map/lqhd,lkhd->lhqk/dot_general | solution.py:124
  377.1 11.6 %fusion = f32[6,16,64]{2,1,0:T(8,128)S(1)} fusion(f32[6,16,64,1024]{3,2,1,0:T(8,128)} %get-tuple-element.31, f32[6,16,64]{2,1,0:T(8,128)S(1)} %broadcast_maximum_fusion), kind=kLoop, calls=%fused_computation.2 | loop fusion | flops 18868224 | bytes 25214976 | tf_op jit(solution)/shard_map/reduce_sum | solution.py:129
  388.7 14.9 %fusion.20 = bf16[6,64,16,72]{3,1,2,0:T(8,128)(2,1)S(1)} fusion(bf16[6,1024,16,72]{1,3,2,0:T(8,128)(2,1)} %bitcast.49, f32[6,16,64,1024]{3,2,1,0:T(8,128)} %get-tuple-element.31, f32[6,16,64]{2,1,0:T(8,128)S(1)} %broadcast_maximum_fusion, f32[6,64,16]{1,2,0:T(8,128)S(1)} %bitcast.56), kind=kOutput, calls=%fused_computation.25 | convolution fusion | flops 925728768 | bytes 40255488 | tf_op jit(solution)/shard_map/lhqk,lkhd->lhqd/dot_general | solution.py:130
  403.6 2.3 copy.30
  405.9 3.2 convert_element_type.64
  409.2 3.4 fusion.63
  414.2 16.7 %all-gather.16.cloned.1.call-done = bf16[1152,4608]{0,1:T(8,128)(2,1)} async-done(((bf16[1152,288]{0,1:T(8,128)(2,1)}), bf16[1152,4608]{0,1:T(8,128)(2,1)}) %all-gather.16.cloned.1.call-update) | async-done | bytes 10616848 | tf_op jit(solution)/shard_map/all_gather | solution.py:147
  430.9 82.7 %all-gather.18.cloned.1.call-done = bf16[4608,1152]{1,0:T(8,128)(2,1)} async-done(((bf16[288,1152]{1,0:T(8,128)(2,1)}), bf16[4608,1152]{1,0:T(8,128)(2,1)}) %all-gather.18.cloned.1.call-update) | async-done | bytes 10616848 | tf_op jit(solution)/shard_map/all_gather | solution.py:148
  513.6 17.6 %fusion.14 = f32[384,1152]{1,0:T(8,128)} fusion(bf16[4608,1152]{1,0:T(8,128)(2,1)} %all-gather.18.cloned.1.call-done, bf16[384,1152]{1,0:T(8,128)(2,1)S(1)} %bitcast.54, bf16[1152,4608]{0,1:T(8,128)(2,1)} %all-gather.16.cloned.1.call-done), kind=kOutput, calls=%fused_computation.17 | convolution fusion | flops 8169652224 | bytes 23887872 | tf_op jit(solution)/shard_map/dot_general | solution.py:153
  531.3 2.5 fusion.59
  (63 shorter events, 11.5 us)
Async XLA Ops:
  6.5 44.8 %copy-start = (bf16[1001,1152]{1,0:T(8,128)(2,1)S(1)}, bf16[1001,1152]{1,0:T(8,128)(2,1)}, u32[]{:S(2)}) copy-start(bf16[1001,1152]{1,0:T(8,128)(2,1)} %param.23) | copy-start | bytes 6918916
  6.5 3.2 copy-start.6
  6.5 42.0 %all-gather.8.cloned.1.call-start = ((), (), s32[]{:S(2)}) async-start(), calls=%async_computation | async-start | bytes 3317760 | tf_op jit(solution)/shard_map/all_gather | solution.py:85
  7.3 113.1 %all-gather.10.cloned.1.call-start = ((), (), s32[]{:S(2)}) async-start(), calls=%async_computation.1 | async-start | bytes 8460288 | tf_op jit(solution)/shard_map/all_gather | solution.py:105
  8.0 292.4 %all-gather.12.cloned.1.call-start = ((), (), s32[]{:S(2)}) async-start(), calls=%async_computation.2 | async-start | bytes 30081024 | tf_op jit(solution)/shard_map/all_gather | solution.py:116
  9.5 3.0 copy-start.5
  9.7 15.3 %copy-start.10 = (s32[6]{0:T(128)S(1)}, s32[6]{0:T(128)}, u32[]{:S(2)}) copy-start(s32[6]{0:T(128)} %param.18) | copy-start | bytes 76
  11.0 1.2 copy-start.2
  53.5 21.2 %copy-start.3 = (f32[6,64,1152]{2,1,0:T(8,128)S(1)}, f32[6,64,1152]{2,1,0:T(8,128)}, u32[]{:S(2)}) copy-start(f32[6,64,1152]{2,1,0:T(8,128)} %copy-done.2) | copy-start | bytes 5308420
  130.3 278.9 %all-gather.14.cloned.1.call-start = ((), (), s32[]{:S(2)}) async-start(), calls=%async_computation.3 | async-start | bytes 2820096 | tf_op jit(solution)/shard_map/all_gather | solution.py:106
  130.9 300.0 %all-gather.16.cloned.1.call-start = ((), (), s32[]{:S(2)}) async-start(), calls=%async_computation.4 | async-start | bytes 11280384 | tf_op jit(solution)/shard_map/all_gather | solution.py:147
  131.5 382.2 %all-gather.18.cloned.1.call-start = ((), (), s32[]{:S(2)}) async-start(), calls=%async_computation.5 | async-start | bytes 11280384 | tf_op jit(solution)/shard_map/all_gather | solution.py:148
  412.6 1.2 copy-start.4
  531.2 2.9 copy-start.9
  531.3 5.7 %copy-start.1 = (bf16[1001,1152]{1,0:T(8,128)(2,1)S(1)}, bf16[1001,1152]{1,0:T(8,128)(2,1)}, u32[]{:S(2)}) copy-start(bf16[1001,1152]{1,0:T(8,128)(2,1)} %param.23) | copy-start | bytes 6918916
  533.8 2.5 copy-start.7
  533.8 2.5 copy-start.8
  534.7 1.6 collective-permute-start
Sparse Core Ops, SparseCore 0:
  9.0 39.5 all-gather.7
  50.7 69.6 all-gather.9
  130.4 169.9 all-gather.11
  302.4 45.8 all-gather.13
  350.3 80.5 all-gather.15
  432.9 80.6 all-gather.17
